TPU v7x, 32 devices: a whole 2x2x4 slice. The times are simulated.
32 devices in a mesh: dp: 2 (over core), ctx: 4 (over z), vocab: 4 (over y, x).
Axes of the slice: x: 2, y: 2, z: 4, core: 2. Of those that a mesh axis runs over, the one named last changes fastest.
Arguments:
- hidden: bfloat16 [512, 4096], P(('dp', 'ctx')), may hold values from -32 to 32
- head_weight: bfloat16 [4096, 9504], P(None, ('ctx', 'vocab')), may hold values from -2 to 2
- targets: int32 [512], P('dp'), may hold values from 0 to 9503
- segment_ids: int32 [512], P('dp'), may hold values from 0 to 31, as said below
- lengths: int32 [32], replicated, may hold values from 8 to 24, as said below
- loss_mask: int32 [512], P('dp'), may hold values 0 or 1
- advantages: float32 [32], replicated, may hold values from -4 to 4
- ref_logprobs: float32 [512], P('dp'), may hold values from -40 to -2
Outputs:
- grad_hidden: bfloat16 [512, 4096], P(('dp', 'ctx', 'vocab'))
- grad_head: bfloat16 [4096, 9504], P(None, ('ctx', 'vocab'))
Inputs may be any that keep to these rules, and one draw needn't show every extreme that they name: `segment_ids`: each sequence's tokens are contiguous; the tokens b * 64 to (b + 1) * 64 - 1 carry ids b * 4 to (b + 1) * 4 - 1, never falling, each id used. lengths[s] is the number of tokens whose segment id is s.
All inputs are finite; a program needn't handle non-finite values. No bound on the sum of `loss_mask` on one device may be relied on, other than what follows from the above.
Results may differ from a plain program's by a relative error of at most 0.012.
Values may be sent and summed in bfloat16 or wider, within the bound.
A program may use at most 128 MiB of HBM per device.

v0:
```python
import jax
import jax.numpy as jnp
from jax import lax
from jax.sharding import PartitionSpec as P

LOSS_SCALE = 1024
kl_weight = 0.1
entropy_weight = 0.05


def per_device(
    hidden, head_weight, targets, segment_ids, lengths, loss_mask, advantages, ref_logprobs
):
    vocab_width = head_weight.shape[1]
    first_column = (
        lax.axis_index("ctx") * lax.axis_size("vocab") + lax.axis_index("vocab")
    ) * vocab_width
    gathered = lax.all_gather(hidden, "ctx", axis=0, tiled=True)
    logits = jnp.dot(gathered, head_weight, preferred_element_type=jnp.float32)
    columns = first_column + lax.iota(jnp.int32, vocab_width)
    target_hits = targets[:, None] == columns[None, :]
    target_part = jnp.sum(jnp.where(target_hits, logits, 0.0), axis=1)
    row_max = lax.pmax(jnp.max(logits, axis=1), ("ctx", "vocab"))
    shifted = jnp.exp(logits - row_max[:, None])
    exp_total, exp_logit, target_logit = lax.psum(
        (jnp.sum(shifted, axis=1), jnp.sum(shifted * logits, axis=1), target_part), ("ctx", "vocab")
    )
    log_total = row_max + jnp.log(exp_total)
    target_logp = target_logit - log_total
    mean_logit = exp_logit / exp_total
    probs = jnp.exp(logits - log_total[:, None])
    seq_onehot = segment_ids[:, None] == lax.iota(jnp.int32, advantages.shape[0])[None, :]
    token_adv = jnp.sum(jnp.where(seq_onehot, advantages[None, :], 0.0), axis=1)
    token_len = jnp.sum(jnp.where(seq_onehot, lengths[None, :].astype(jnp.float32), 0.0), axis=1)
    token_weight = LOSS_SCALE * loss_mask.astype(jnp.float32) / token_len
    logp_grad = -token_adv + kl_weight * (target_logp - ref_logprobs)
    inner = logp_grad[:, None] * (target_hits.astype(jnp.float32) - probs)
    inner = inner + entropy_weight * probs * (logits - mean_logit[:, None])
    grad_logits = (token_weight[:, None] * inner).astype(jnp.bfloat16)
    head_local = lax.dot_general(
        gathered, grad_logits, (((0,), (0,)), ((), ())), preferred_element_type=jnp.float32
    ).astype(jnp.bfloat16)
    grad_head = lax.psum(head_local, "dp").astype(jnp.float32).astype(jnp.bfloat16)
    grad_hidden = lax.psum_scatter(
        lax.dot_general(
            grad_logits, head_weight, (((1,), (1,)), ((), ())), preferred_element_type=jnp.float32
        ),
        ("ctx", "vocab"),
        scatter_dimension=0,
        tiled=True,
    )
    return (grad_hidden.astype(jnp.bfloat16), grad_head)


def solution(mesh):
    return jax.shard_map(
        per_device,
        mesh=mesh,
        in_specs=(
            P(("dp", "ctx"), None),
            P(None, ("ctx", "vocab")),
            P("dp"),
            P("dp"),
            P(),
            P("dp"),
            P(),
            P("dp"),
        ),
        out_specs=(P(("dp", "ctx", "vocab"), None), P(None, ("ctx", "vocab"))),
        check_vma=False,
    )
```

profile of v0, /device:TPU:0, one launch (start us, length us, event | category | flops | bytes accessed | tf_op | source)
XLA Modules:
  0.0 282.1 jit_solution(3857916356808033694)
XLA Ops:
  7.2 0.0 all-gather.2.cloned.1.call-start
  7.2 0.7 all-gather.2.cloned.1.call-update
  7.9 0.0 reduce-scatter.2.cloned.1.call-start
  7.9 0.7 convert_element_type.25
  8.6 0.8 select_reduce_fusion.1
  9.4 0.7 multiply_divide_fusion
  10.1 0.0 copy-start.1
  10.1 0.0 copy-start.2
  10.1 47.9 %all-gather.2.cloned.1.call-done = bf16[256,4096]{1,0:T(8,128)(2,1)} async-done(((bf16[64,4096]{1,0:T(8,128)(2,1)}), bf16[256,4096]{1,0:T(8,128)(2,1)}) %all-gather.2.cloned.1.call-update) | async-done | bytes 2097168 | tf_op jit(solution)/shard_map/all_gather | solution.py:18
  58.0 4.5 %fusion.11 = (f32[256]{0:T(256)S(1)}, f32[256,594]{0,1:T(8,128)S(1)}) fusion(bf16[256,4096]{1,0:T(8,128)(2,1)} %all-gather.2.cloned.1.call-done, bf16[4096,594]{0,1:T(8,128)(2,1)} %param.9), kind=kOutput, calls=%fused_computation.21 | convolution fusion | flops 1245860096 | bytes 7572480 | tf_op jit(solution)/shard_map/dot_general | solution.py:19
  62.5 39.5 %pmax.7 = f32[256]{0:T(256)S(1)} all-reduce(f32[256]{0:T(256)S(1)} %get-tuple-element.13), channel_id=1, replica_groups=mesh['dp'=2,'ctx'=4,'vocab'=4] {'ctx','vocab'}, use_global_device_ids=true, to_apply=%region_5.6 | all-reduce | flops 256 | bytes 2048 | tf_op jit(solution)/shard_map/pmax | solution.py:23
  102.0 0.0 copy-done.1
  102.0 0.2 fusion.7
  102.2 36.6 %all-reduce = (f32[256]{0:T(256)S(1)}, f32[256]{0:T(256)S(1)}, f32[256]{0:T(256)S(1)}) all-reduce(f32[256]{0:T(256)S(1)} %get-tuple-element.3, f32[256]{0:T(256)S(1)} %get-tuple-element.2, f32[256]{0:T(256)S(1)} %get-tuple-element.4), channel_id=1, replica_groups=mesh['dp'=2,'ctx'=4,'vocab'=4] {'ctx','vocab'}, use_global_device_ids=true, to_apply=%region_9.10 | all-reduce | flops 768 | bytes 6144 | tf_op jit(solution)/shard_map/psum | solution.py:25
  138.8 0.0 copy-done.2
  138.8 6.5 %fusion.9 = f32[256,4096]{1,0:T(8,128)} fusion(bf16[4096,594]{0,1:T(8,128)(2,1)} %param.9, f32[256,594]{0,1:T(8,128)S(1)} %get-tuple-element.14, f32[256]{0:T(256)S(1)} %get-tuple-element.12, f32[256]{0:T(256)S(1)} %get-tuple-element.11, f32[256]{0:T(256)S(1)} %get-tuple-element.10, s32[256]{0:T(256)S(1)} %copy-done.1, f32[256]{0:T(256)S(1)} %multiply_divide_fusion, ...), kind=kOutput, calls=%fused_computation.20 | convolution fusion | flops 1247380992 | bytes 9676104 | tf_op jit(solution)/shard_map/dot_general | solution.py:45
  145.3 0.0 copy-start
  145.3 0.0 reduce-scatter.2.cloned.1.call-update
  145.3 0.0 all-reduce.3.cloned.1.call-start
  145.4 1.5 copy-done
  146.9 3.9 %fusion = bf16[4096,594]{0,1:T(8,128)(2,1)} fusion(bf16[256,4096]{1,0:T(8,128)(2,1)S(1)} %copy-done, f32[256,594]{0,1:T(8,128)S(1)} %get-tuple-element.14, f32[256]{0:T(256)S(1)} %get-tuple-element.12, f32[256]{0:T(256)S(1)} %get-tuple-element.11, f32[256]{0:T(256)S(1)} %get-tuple-element.10, s32[256]{0:T(256)S(1)} %copy-done.1, ...), kind=kOutput, calls=%fused_computation.1 | convolution fusion | flops 1249814016 | bytes 7578952 | tf_op jit(solution)/shard_map/dot_general | solution.py:40
  150.7 0.0 all-reduce.3.cloned.1.call-update
  150.8 87.7 %reduce-scatter.2.cloned.1.call-done = f32[16,4096]{1,0:T(8,128)} async-done(((f32[256,4096]{1,0:T(8,128)}), f32[16,4096]{1,0:T(8,128)}) %reduce-scatter.2.cloned.1.call-update) | async-done | bytes 262160 | tf_op jit(solution)/shard_map/reduce_scatter | solution.py:44
  238.5 1.6 convert_element_type.28
  240.1 30.2 %all-reduce.3.cloned.1.call-done = bf16[4096,594]{0,1:T(8,128)(2,1)} async-done(((bf16[4096,594]{0,1:T(8,128)(2,1)}), bf16[4096,594]{0,1:T(8,128)(2,1)}) %all-reduce.3.cloned.1.call-update) | async-done | bytes 4866064 | tf_op jit(solution)/shard_map/psum | solution.py:43
  270.3 5.2 %copy.11 = bf16[4096,594]{0,1:T(8,128)(2,1)} copy(bf16[4096,594]{0,1:T(8,128)(2,1)} %all-reduce.3.cloned.1.call-done) | data formatting | bytes 9732096
  (2 shorter events, 0.0 us)
Async XLA Ops:
  7.2 50.8 %all-gather.2.cloned.1.call-start = ((), (), s32[]{:S(2)}) async-start(), calls=%async_computation.1 | async-start | bytes 2621440 | tf_op jit(solution)/shard_map/all_gather | solution.py:18
  7.9 230.6 %reduce-scatter.2.cloned.1.call-start = ((), (), s32[]{:S(2)}) async-start(), calls=%async_computation.2 | async-start | bytes 4456448 | tf_op jit(solution)/shard_map/reduce_scatter | solution.py:44
  10.1 91.9 %copy-start.1 = (s32[256]{0:T(256)S(1)}, s32[256]{0:T(256)}, u32[]{:S(2)}) copy-start(s32[256]{0:T(256)} %param.10) | copy-start | bytes 3076
  10.1 128.7 %copy-start.2 = (f32[256]{0:T(256)S(1)}, f32[256]{0:T(256)}, u32[]{:S(2)}) copy-start(f32[256]{0:T(256)} %param.15) | copy-start | bytes 3076
  145.3 1.6 copy-start
  145.3 125.0 %all-reduce.3.cloned.1.call-start = ((), (), s32[]{:S(2)}) async-start(), calls=%async_computation.3 | async-start | bytes 9830400 | tf_op jit(solution)/shard_map/psum | solution.py:43
Sparse Core Ops, SparseCore 0:
  9.5 48.3 all-gather.1
  145.4 93.0 reduce-scatter.1
  241.6 28.6 all-reduce.2
where the time goes:
time: 282 us
  waiting for transfers between devices  167 us (59%)
  blocking collectives  76.1 us (27%)
  matrix products  14.9 us (5%)
  between operations  13.8 us (5%)
  local copies, waits for them, and re-layouts  6.77 us (2%)
  other arithmetic  3.95 us (1%)
    reduce_scatter x1, waiting for transfers between devices, per_device(): lax.psum_scatter(lax.dot_general(grad_logits, head_weight, (((1,), (1,)),...  87.7 us
    all_gather x1, waiting for transfers between devices, per_device(): gathered = lax.all_gather(hidden, 'ctx', axis=0, tiled=True)  47.9 us
    pmax x1, blocking collectives, per_device(): row_max = lax.pmax(jnp.max(logits, axis=1), ('ctx', 'vocab'))  39.5 us
    psum x1, blocking collectives, per_device(): lax.psum((jnp.sum(shifted, axis=1), jnp.sum(shifted * logits, axis=1), ta...  36.6 us
    psum x1, waiting for transfers between devices, per_device(): lax.psum(head_local, 'dp').astype(jnp.float32).astype(jnp.bfloat16)  30.2 us
    unnamed x7, local copies, waits for them, and re-layouts  6.77 us
    dot_general x1, matrix products, per_device(): lax.dot_general(grad_logits, head_weight, (((1,), (1,)), ((), ())), prefe...  6.48 us
  transfers between devices with their start and end apart: 3, of which 3 were waited for; matrix products, arithmetic and copies ran while one was open for 3% of the time, Pallas kernels for 0%

commit v1 on v0

--- a/solution.py
+++ b/solution.py
@@ -15,7 +15,18 @@
     first_column = (
         lax.axis_index("ctx") * lax.axis_size("vocab") + lax.axis_index("vocab")
     ) * vocab_width
-    gathered = lax.all_gather(hidden, "ctx", axis=0, tiled=True)
+    n_blocks = jax.lax.axis_size("ctx")
+    sheets = [hidden]
+    for k0 in range(n_blocks - 1):
+        sheets.append(
+            jax.lax.ppermute(
+                sheets[-1],
+                axis_name="ctx",
+                perm=[(dev_j, (dev_j + 1) % n_blocks) for dev_j in range(n_blocks)],
+            )
+        )
+    f_now = jnp.concatenate(sheets[::-1], axis=0)
+    gathered = jnp.roll(f_now, (jax.lax.axis_index("ctx") + 1) * hidden.shape[0], 0)
     logits = jnp.dot(gathered, head_weight, preferred_element_type=jnp.float32)
     columns = first_column + lax.iota(jnp.int32, vocab_width)
     target_hits = targets[:, None] == columns[None, :]

time: 282 us -> 246 us (0.87)
  waiting for transfers between devices: 167 us -> 128 us
  starting transfers between devices: 0.12 us -> 3.19 us
    all_gather x1 -> x0, waiting for transfers between devices: 47.9 us -> none  [per_device(): gathered = lax.all_gather(hidden, 'ctx', axis=0, tiled=True)]
    ppermute x0 -> x3, waiting for transfers between devices: none -> 41 us  [per_device(): jax.lax.ppermute(sheets[-1], axis_name='ctx', perm=[(dev_j, (dev_j + 1) %...]
    psum x1, waiting for transfers between devices: 30.2 us -> 0.01 us  [per_device(): lax.psum(head_local, 'dp').astype(jnp.float32).astype(jnp.bfloat16)]
    ppermute x0 -> x3, starting transfers between devices: none -> 3.11 us  [per_device(): jax.lax.ppermute(sheets[-1], axis_name='ctx', perm=[(dev_j, (dev_j + 1) %...]
    dot_general x1, matrix products: 4.53 us -> 1.63 us  [per_device(): logits = jnp.dot(gathered, head_weight, preferred_element_type=jnp.float32)]
    unnamed x7 -> x18, local copies, waits for them, and re-layouts: 6.77 us -> 6.82 us
  transfers between devices with their start and end apart: 3 -> 5, of which waited for: 3 -> 4; matrix products, arithmetic and copies ran while one was open for 3% -> 4% of each run, Pallas kernels for 0% -> 0%
where the time goes in v1:
time: 246 us
  waiting for transfers between devices  128 us (52%)
  blocking collectives  75.2 us (31%)
  between operations  15.6 us (6%)
  matrix products  13.5 us (5%)
  local copies, waits for them, and re-layouts  6.86 us (3%)
  other arithmetic  3.95 us (2%)
  starting transfers between devices  3.19 us (1%)
    reduce_scatter x1, waiting for transfers between devices, per_device(): lax.psum_scatter(lax.dot_general(grad_logits, head_weight, (((1,), (1,)),...  86.7 us
    ppermute x3, waiting for transfers between devices, per_device(): jax.lax.ppermute(sheets[-1], axis_name='ctx', perm=[(dev_j, (dev_j + 1) %...  41 us
    pmax x1, blocking collectives, per_device(): row_max = lax.pmax(jnp.max(logits, axis=1), ('ctx', 'vocab'))  37.6 us
    psum x1, blocking collectives, per_device(): lax.psum((jnp.sum(shifted, axis=1), jnp.sum(shifted * logits, axis=1), ta...  37.5 us
    unnamed x18, local copies, waits for them, and re-layouts  6.82 us
    dot_general x1, matrix products, per_device(): lax.dot_general(grad_logits, head_weight, (((1,), (1,)), ((), ())), prefe...  6.47 us
    dot_general x1, matrix products, per_device(): lax.dot_general(gathered, grad_logits, (((0,), (0,)), ((), ())), preferre...  5.41 us
  transfers between devices with their start and end apart: 5, of which 4 were waited for; matrix products, arithmetic and copies ran while one was open for 4% of the time, Pallas kernels for 0%

profile of v1, /device:TPU:0, one launch (start us, length us, event | category | flops | bytes accessed | tf_op | source)
XLA Modules:
  0.0 246.0 jit_solution(9360287773270463425)
XLA Ops:
  8.0 0.0 copy-start.1
  8.0 0.0 reduce-scatter.2.cloned.1.call-start
  8.1 3.1 %collective-permute-start = (bf16[64,4096]{1,0:T(8,128)(2,1)}, bf16[64,4096]{1,0:T(8,128)(2,1)S(1)}, u32[]{:S(2)}, u32[]{:S(2)}) collective-permute-start(bf16[64,4096]{1,0:T(8,128)(2,1)} %param.8), channel_id=1, source_target_pairs={{0,4},{4,8},{8,12},{12,0},{1,5},{5,9},{9,13},{13,1},{2,6},{6,10},{... | collective-permute-start | bytes 1572872 | tf_op jit(solution)/shard_map/ppermute | solution.py:22
  11.2 14.2 %collective-permute-done = bf16[64,4096]{1,0:T(8,128)(2,1)S(1)} collective-permute-done((bf16[64,4096]{1,0:T(8,128)(2,1)}, bf16[64,4096]{1,0:T(8,128)(2,1)S(1)}, u32[]{:S(2)}, u32[]{:S(2)}) %collective-permute-start) | collective-permute-done | bytes 524320 | tf_op jit(solution)/shard_map/ppermute | solution.py:22
  25.3 0.0 collective-permute-start.1
  25.3 14.9 %collective-permute-done.1 = bf16[64,4096]{1,0:T(8,128)(2,1)S(1)} collective-permute-done((bf16[64,4096]{1,0:T(8,128)(2,1)S(1)}, bf16[64,4096]{1,0:T(8,128)(2,1)S(1)}, u32[]{:S(2)}, u32[]{:S(2)}) %collective-permute-start.1) | collective-permute-done | bytes 524320 | tf_op jit(solution)/shard_map/ppermute | solution.py:22
  40.2 0.0 collective-permute-start.2
  40.2 0.7 convert_element_type.22
  40.9 0.8 select_reduce_fusion.1
  41.6 0.7 multiply_divide_fusion
  42.3 0.0 copy-start
  42.3 11.9 %collective-permute-done.2 = bf16[64,4096]{1,0:T(8,128)(2,1)S(1)} collective-permute-done((bf16[64,4096]{1,0:T(8,128)(2,1)S(1)}, bf16[64,4096]{1,0:T(8,128)(2,1)S(1)}, u32[]{:S(2)}, u32[]{:S(2)}) %collective-permute-start.2) | collective-permute-done | bytes 524320 | tf_op jit(solution)/shard_map/ppermute | solution.py:22
  54.4 1.1 constant_dynamic-update-slice_fusion.4
  55.6 0.0 copy-done.1
  55.6 0.0 copy-done
  55.6 0.0 copy-start.2
  55.7 0.0 copy-start.3
  55.7 0.0 copy-start.4
  55.7 1.6 fusion.15
  57.3 0.3 copy-done.2
  57.6 37.6 %pmax.7 = f32[256]{0:T(256)S(1)} all-reduce(f32[256]{0:T(256)S(1)} %get-tuple-element.13), channel_id=1, replica_groups=mesh['dp'=2,'ctx'=4,'vocab'=4] {'ctx','vocab'}, use_global_device_ids=true, to_apply=%region_5.6 | all-reduce | flops 256 | bytes 2048 | tf_op jit(solution)/shard_map/pmax | solution.py:34
  95.2 0.0 copy-done.3
  95.2 0.2 fusion.9
  95.4 37.5 %all-reduce = (f32[256]{0:T(256)S(1)}, f32[256]{0:T(256)S(1)}, f32[256]{0:T(256)S(1)}) all-reduce(f32[256]{0:T(256)S(1)} %get-tuple-element.3, f32[256]{0:T(256)S(1)} %get-tuple-element.2, f32[256]{0:T(256)S(1)} %get-tuple-element.4), channel_id=1, replica_groups=mesh['dp'=2,'ctx'=4,'vocab'=4] {'ctx','vocab'}, use_global_device_ids=true, to_apply=%region_9.10 | all-reduce | flops 768 | bytes 6144 | tf_op jit(solution)/shard_map/psum | solution.py:36
  132.9 0.0 copy-done.4
  133.0 6.5 %fusion.13 = f32[256,4096]{1,0:T(8,128)} fusion(bf16[4096,594]{0,1:T(8,128)(2,1)} %param.9, f32[256,594]{0,1:T(8,128)S(1)} %get-tuple-element.14, f32[256]{0:T(256)S(1)} %get-tuple-element.12, f32[256]{0:T(256)S(1)} %get-tuple-element.11, f32[256]{0:T(256)S(1)} %get-tuple-element.10, s32[256]{0:T(256)S(1)} %copy-done.3, f32[256]{0:T(256)S(1)} %multiply_divide_fusion, ...), kind=kOutput, calls=%fused_computation.32 | convolution fusion | flops 1247380992 | bytes 9676104 | tf_op jit(solution)/shard_map/dot_general | solution.py:56
  139.4 0.0 reduce-scatter.2.cloned.1.call-update
  139.5 0.0 all-reduce.3.cloned.1.call-start
  139.5 5.4 %convolution_convert_fusion = bf16[4096,594]{0,1:T(8,128)(2,1)} fusion(bf16[512,4096]{1,0:T(8,128)(2,1)} %copy-done.2, s32[]{:T(128)S(6)} %select_n.27, f32[256,594]{0,1:T(8,128)S(1)} %get-tuple-element.14, f32[256]{0:T(256)S(1)} %get-tuple-element.12, f32[256]{0:T(256)S(1)} %get-tuple-element.11, f32[256]{0:T(256)S(1)} %get-tuple-element.10, ...), kind=kOutput, calls=%fused_computation | convolution fusion | flops 1249814016 | bytes 7578956 | tf_op jit(solution)/shard_map/dot_general | solution.py:51
  144.9 0.0 all-reduce.3.cloned.1.call-update
  144.9 86.7 %reduce-scatter.2.cloned.1.call-done = f32[16,4096]{1,0:T(8,128)} async-done(((f32[256,4096]{1,0:T(8,128)}), f32[16,4096]{1,0:T(8,128)}) %reduce-scatter.2.cloned.1.call-update) | async-done | bytes 262160 | tf_op jit(solution)/shard_map/reduce_scatter | solution.py:55
  231.6 1.6 convert_element_type.25
  233.3 0.0 all-reduce.3.cloned.1.call-done
  233.3 5.2 %copy.18 = bf16[4096,594]{0,1:T(8,128)(2,1)} copy(bf16[4096,594]{0,1:T(8,128)(2,1)} %all-reduce.3.cloned.1.call-done) | data formatting | bytes 9732096
  (9 shorter events, 0.3 us)
Async XLA Ops:
  8.0 47.6 %copy-start.1 = (bf16[64,4096]{1,0:T(8,128)(2,1)S(1)}, bf16[64,4096]{1,0:T(8,128)(2,1)}, u32[]{:S(2)}) copy-start(bf16[64,4096]{1,0:T(8,128)(2,1)} %param.8) | copy-start | bytes 1572868
  8.0 223.6 %reduce-scatter.2.cloned.1.call-start = ((), (), s32[]{:S(2)}) async-start(), calls=%async_computation.1 | async-start | bytes 4456448 | tf_op jit(solution)/shard_map/reduce_scatter | solution.py:55
  8.1 17.3 %collective-permute-start = (bf16[64,4096]{1,0:T(8,128)(2,1)}, bf16[64,4096]{1,0:T(8,128)(2,1)S(1)}, u32[]{:S(2)}, u32[]{:S(2)}) collective-permute-start(bf16[64,4096]{1,0:T(8,128)(2,1)} %param.8), channel_id=1, source_target_pairs={{0,4},{4,8},{8,12},{12,0},{1,5},{5,9},{9,13},{13,1},{2,6},{6,10},{... | collective-permute-start | bytes 1572872 | tf_op jit(solution)/shard_map/ppermute | solution.py:22
  25.3 14.9 %collective-permute-start.1 = (bf16[64,4096]{1,0:T(8,128)(2,1)S(1)}, bf16[64,4096]{1,0:T(8,128)(2,1)S(1)}, u32[]{:S(2)}, u32[]{:S(2)}) collective-permute-start(bf16[64,4096]{1,0:T(8,128)(2,1)S(1)} %collective-permute-done), channel_id=1, source_target_pairs={{0,4},{4,8},{8,12},{12,0},{1,5},{5,9},{9,13},{13,1},{2,6},{6,10},{... | collective-permute-start | bytes 1572872 | tf_op jit(solution)/shard_map/ppermute | solution.py:22
  40.2 14.0 %collective-permute-start.2 = (bf16[64,4096]{1,0:T(8,128)(2,1)S(1)}, bf16[64,4096]{1,0:T(8,128)(2,1)S(1)}, u32[]{:S(2)}, u32[]{:S(2)}) collective-permute-start(bf16[64,4096]{1,0:T(8,128)(2,1)S(1)} %collective-permute-done.1), channel_id=1, source_target_pairs={{0,4},{4,8},{8,12},{12,0},{1,5},{5,9},{9,13},{13,1},{2,6},{6,10},{... | collective-permute-start | bytes 1572872 | tf_op jit(solution)/shard_map/ppermute | solution.py:22
  42.3 13.3 %copy-start = (bf16[4096,594]{0,1:T(8,128)(2,1)S(1)}, bf16[4096,594]{0,1:T(8,128)(2,1)}, u32[]{:S(2)}) copy-start(bf16[4096,594]{0,1:T(8,128)(2,1)} %param.9) | copy-start | bytes 14598148
  55.6 1.9 copy-start.2
  55.7 39.6 %copy-start.3 = (s32[256]{0:T(256)S(1)}, s32[256]{0:T(256)}, u32[]{:S(2)}) copy-start(s32[256]{0:T(256)} %param.10) | copy-start | bytes 3076
  55.7 77.3 %copy-start.4 = (f32[256]{0:T(256)S(1)}, f32[256]{0:T(256)}, u32[]{:S(2)}) copy-start(f32[256]{0:T(256)} %param.15) | copy-start | bytes 3076
  139.5 93.8 %all-reduce.3.cloned.1.call-start = ((), (), s32[]{:S(2)}) async-start(), calls=%async_computation.2 | async-start | bytes 9830400 | tf_op jit(solution)/shard_map/psum | solution.py:54
Sparse Core Ops, SparseCore 0:
  139.6 92.0 reduce-scatter.1
Sparse Core Ops, SparseCore 1:
  145.0 25.4 all-reduce.2
